TPU v7x, 512 devices: a whole 4x8x8 slice. The times are simulated.
512 devices in a mesh: tok: 8 (over z), wid: 64 (over x, y, core).
Axes of the slice: x: 4, y: 8, z: 8, core: 2. Of those that a mesh axis runs over, the one named last changes fastest.
Arguments:
- tokens: bfloat16 [1536, 4096], P('tok', 'wid'), may hold values from -80 to 80
- gate_a: bfloat16 [16384, 4096], P('wid', 'tok'), may hold values from -0.09375 to 0.09375
- up_a: bfloat16 [16384, 4096], P('wid', 'tok'), may hold values from -0.09375 to 0.09375
- gate_b: bfloat16 [16384, 4096], P('wid', 'tok'), may hold values from -0.09375 to 0.09375
- up_b: bfloat16 [16384, 4096], P('wid', 'tok'), may hold values from -0.09375 to 0.09375
- down_a: bfloat16 [16384, 4096], P('wid', 'tok'), may hold values from -0.125 to 0.125
- down_b: bfloat16 [16384, 4096], P('wid', 'tok'), may hold values from -0.125 to 0.125
- block_perm: int32 [128], replicated, may hold values from 0 to 127, each once
Outputs:
- merged: bfloat16 [1536, 4096], P('tok', 'wid')
Inputs may be any that keep to these rules, and one draw needn't show every extreme that they name: block_perm names every block number once.
All inputs are finite; a program needn't handle non-finite values.
Results may differ from a plain program's by a relative error of at most 0.0058.
Values may be sent and summed in bfloat16 or wider, within the bound.
A program may use at most 64 MiB of HBM per device.

v0:
```python
import jax
import jax.numpy as jnp
from jax import lax
from jax.sharding import PartitionSpec as P

FF = 16384
BLOCK = 128


def sigmoid_linear(preact):
    return preact / (1.0 + jnp.exp(-preact))


def reorder_blocks(matrix_in, block_perm):
    shaped = matrix_in.reshape(FF // BLOCK, BLOCK, matrix_in.shape[1])
    return jnp.take(shaped, block_perm, axis=0).reshape(matrix_in.shape)


def add_products(pieces, gathered):
    return tuple(
        (
            lax.dot_general(
                gathered, piece, (((1,), (1,)), ((), ())), preferred_element_type=jnp.float32
            )
            for piece in pieces
        )
    )


def local(tokens, gate_a, up_a, gate_b, up_b, down_a, down_b, block_perm):
    gathered = lax.all_gather(tokens, "wid", axis=1, tiled=True)
    row_count = gathered.shape[0]
    shipped = (
        lax.all_to_all(gate_b, "wid", split_axis=1, concat_axis=0, tiled=True),
        lax.all_to_all(up_b, "wid", split_axis=1, concat_axis=0, tiled=True),
        lax.all_to_all(down_b, "wid", split_axis=1, concat_axis=0, tiled=True),
    )
    gate_src, up_src, down_perm = (
        lax.all_to_all(
            reorder_blocks(shipped[0], block_perm), "wid", split_axis=0, concat_axis=1, tiled=True
        ),
        lax.all_to_all(
            reorder_blocks(shipped[1], block_perm), "wid", split_axis=0, concat_axis=1, tiled=True
        ),
        lax.all_to_all(
            reorder_blocks(shipped[2], block_perm), "wid", split_axis=0, concat_axis=1, tiled=True
        ),
    )
    gate_av, up_av, gate_bv, up_bv = add_products(
        (
            lax.all_gather(gate_a, "tok", axis=1, tiled=True),
            lax.all_gather(up_a, "tok", axis=1, tiled=True),
            lax.all_gather(gate_src, "tok", axis=1, tiled=True),
            lax.all_gather(up_src, "tok", axis=1, tiled=True),
        ),
        gathered,
    )
    hid_a = sigmoid_linear(gate_av) * up_av
    hid_b = sigmoid_linear(gate_bv) * up_bv
    hid_m = sigmoid_linear(0.5 * (gate_av + gate_bv)) * (0.5 * (up_av + up_bv))
    token_total = row_count * lax.axis_size("tok")
    totals = lax.psum(
        (jnp.sum(hid_a, axis=0), jnp.sum(hid_b, axis=0), jnp.sum(hid_m, axis=0)), "tok"
    )
    centers = tuple((total / token_total for total in totals))
    squares = lax.psum(
        (
            jnp.sum((hid_a - centers[0]) ** 2, axis=0),
            jnp.sum((hid_b - centers[1]) ** 2, axis=0),
            jnp.sum((hid_m - centers[2]) ** 2, axis=0),
        ),
        "tok",
    )
    spreads = tuple((square / token_total for square in squares))
    deviations = tuple((jnp.sqrt(spread + 1e-05) for spread in spreads))
    target_std = 0.5 * (deviations[0] + deviations[1])
    target_mean = 0.5 * (centers[0] + centers[1])
    repaired = ((hid_m - centers[2]) / deviations[2] * target_std + target_mean).astype(
        jnp.bfloat16
    )
    down_mid = ((down_a.astype(jnp.float32) + down_perm.astype(jnp.float32)) * 0.5).astype(
        jnp.bfloat16
    )
    partial_out = jnp.dot(
        repaired,
        lax.all_gather(down_mid, "tok", axis=1, tiled=True),
        preferred_element_type=jnp.float32,
    )
    summed = lax.psum_scatter(partial_out, "wid", scatter_dimension=1, tiled=True)
    return summed.astype(jnp.bfloat16)


def solution(mesh):
    return jax.shard_map(
        local,
        mesh=mesh,
        in_specs=(
            P("tok", "wid"),
            P("wid", "tok"),
            P("wid", "tok"),
            P("wid", "tok"),
            P("wid", "tok"),
            P("wid", "tok"),
            P("wid", "tok"),
            P(),
        ),
        out_specs=P("tok", "wid"),
        check_vma=False,
    )
```

profile of v0, /device:TPU:16, one launch (start us, length us, event | category | flops | bytes accessed | tf_op | source)
XLA Modules:
  0.0 485.1 jit_solution(15461387688074729571)
XLA Ops:
  6.5 0.7 all-gather.7.cloned.1.call-update
  7.3 0.7 all-gather.9.cloned.1.call-update
  8.7 1.8 copy.9
  10.5 10.5 %all-to-all-start = ((bf16[256,64,8]{0,2,1:T(8,128)(2,1)}), bf16[256,64,8]{0,2,1:T(8,128)(2,1)S(1)}, u32[]{:S(2)}, u32[]{:S(2)}) async-start(bf16[256,64,8]{0,2,1:T(8,128)(2,1)} %bitcast), calls=%async_computation | async-start | bytes 524288 | tf_op jit(solution)/shard_map/all_to_all | solution.py:34
  21.0 1.8 copy.10
  22.8 9.9 %all-to-all-done = bf16[256,64,8]{0,2,1:T(8,128)(2,1)S(1)} async-done(((bf16[256,64,8]{0,2,1:T(8,128)(2,1)}), bf16[256,64,8]{0,2,1:T(8,128)(2,1)S(1)}, u32[]{:S(2)}, u32[]{:S(2)}) %all-to-all-start) | async-done | bytes 262176 | tf_op jit(solution)/shard_map/all_to_all | solution.py:34
  32.7 6.3 %all-to-all-start.2 = ((bf16[256,64,8]{0,2,1:T(8,128)(2,1)}), bf16[256,64,8]{0,2,1:T(8,128)(2,1)S(1)}, u32[]{:S(2)}, u32[]{:S(2)}) async-start(bf16[256,64,8]{0,2,1:T(8,128)(2,1)} %bitcast.7), calls=%async_computation.2 | async-start | bytes 524288 | tf_op jit(solution)/shard_map/all_to_all | solution.py:35
  39.0 0.8 copy.12
  39.9 10.8 %all-to-all-done.2 = bf16[256,64,8]{0,2,1:T(8,128)(2,1)S(1)} async-done(((bf16[256,64,8]{0,2,1:T(8,128)(2,1)}), bf16[256,64,8]{0,2,1:T(8,128)(2,1)S(1)}, u32[]{:S(2)}, u32[]{:S(2)}) %all-to-all-start.2) | async-done | bytes 262176 | tf_op jit(solution)/shard_map/all_to_all | solution.py:35
  50.7 6.7 %all-to-all-start.4 = ((bf16[256,64,8]{0,2,1:T(8,128)(2,1)}), bf16[256,64,8]{0,2,1:T(8,128)(2,1)S(1)}, u32[]{:S(2)}, u32[]{:S(2)}) async-start(bf16[256,64,8]{0,2,1:T(8,128)(2,1)} %bitcast.14), calls=%async_computation.4 | async-start | bytes 524288 | tf_op jit(solution)/shard_map/all_to_all | solution.py:36
  57.5 0.7 gather_fusion
  58.9 10.2 %all-to-all-done.4 = bf16[256,64,8]{0,2,1:T(8,128)(2,1)S(1)} async-done(((bf16[256,64,8]{0,2,1:T(8,128)(2,1)}), bf16[256,64,8]{0,2,1:T(8,128)(2,1)S(1)}, u32[]{:S(2)}, u32[]{:S(2)}) %all-to-all-start.4) | async-done | bytes 262176 | tf_op jit(solution)/shard_map/all_to_all | solution.py:36
  69.8 0.9 broadcast_select_fusion.2
  70.8 19.1 %all_to_all.99 = bf16[64,256,8]{1,2,0:T(8,128)(2,1)} all-to-all(bf16[64,256,8]{1,2,0:T(8,128)(2,1)S(1)} %bitcast.48), channel_id=1, replica_groups=mesh['tok'=8,'wid'=64] {'wid'}, dimensions={0} | all-to-all | bytes 524288 | tf_op jit(solution)/shard_map/all_to_all | solution.py:39
  89.9 18.3 %all_to_all.100 = bf16[64,256,8]{1,2,0:T(8,128)(2,1)} all-to-all(bf16[64,256,8]{1,2,0:T(8,128)(2,1)S(1)} %bitcast.47), channel_id=1, replica_groups=mesh['tok'=8,'wid'=64] {'wid'}, dimensions={0} | all-to-all | bytes 524288 | tf_op jit(solution)/shard_map/all_to_all | solution.py:42
  108.2 6.3 %all-to-all-start.5 = ((bf16[64,256,8]{1,2,0:T(8,128)(2,1)}), bf16[64,256,8]{1,2,0:T(8,128)(2,1)S(1)}, u32[]{:S(2)}, u32[]{:S(2)}) async-start(bf16[64,256,8]{1,2,0:T(8,128)(2,1)} %bitcast.17), calls=%async_computation.5 | async-start | bytes 524288 | tf_op jit(solution)/shard_map/all_to_all | solution.py:45
  114.8 11.5 %all-to-all-done.5 = bf16[64,256,8]{1,2,0:T(8,128)(2,1)S(1)} async-done(((bf16[64,256,8]{1,2,0:T(8,128)(2,1)}), bf16[64,256,8]{1,2,0:T(8,128)(2,1)S(1)}, u32[]{:S(2)}, u32[]{:S(2)}) %all-to-all-start.5) | async-done | bytes 262176 | tf_op jit(solution)/shard_map/all_to_all | solution.py:45
  126.3 0.8 fusion.1
  127.2 16.2 %all-gather.9.cloned.1.call-done = bf16[256,4096]{1,0:T(8,128)(2,1)} async-done(((bf16[256,512]{1,0:T(8,128)(2,1)}), bf16[256,4096]{1,0:T(8,128)(2,1)}) %all-gather.9.cloned.1.call-update) | async-done | bytes 2097168 | tf_op jit(solution)/shard_map/all_gather | solution.py:51
  143.4 3.1 fusion.10
  146.4 41.8 %all-gather.13.cloned.1.call-done = bf16[256,4096]{1,0:T(8,128)(2,1)} async-done(((bf16[256,512]{1,0:T(8,128)(2,1)}), bf16[256,4096]{1,0:T(8,128)(2,1)}) %all-gather.13.cloned.1.call-update) | async-done | bytes 2097168 | tf_op jit(solution)/shard_map/all_gather | solution.py:52
  188.2 2.4 fusion.11
  190.7 42.3 %all-gather.11.cloned.1.call-done = bf16[256,4096]{0,1:T(8,128)(2,1)} async-done(((bf16[256,512]{0,1:T(8,128)(2,1)}), bf16[256,4096]{0,1:T(8,128)(2,1)}) %all-gather.11.cloned.1.call-update) | async-done | bytes 2097168 | tf_op jit(solution)/shard_map/all_gather | solution.py:53
  232.9 2.4 convolution_bitcast_fusion.1
  235.4 42.2 %all-gather.15.cloned.1.call-done = bf16[256,4096]{0,1:T(8,128)(2,1)} async-done(((bf16[256,512]{0,1:T(8,128)(2,1)}), bf16[256,4096]{0,1:T(8,128)(2,1)}) %all-gather.15.cloned.1.call-update) | async-done | bytes 2097168 | tf_op jit(solution)/shard_map/all_gather | solution.py:54
  277.6 2.5 fusion.8
  280.1 15.7 %all-reduce.1 = (f32[256]{0:T(256)S(1)}, f32[256]{0:T(256)S(1)}, f32[256]{0:T(256)S(1)}) all-reduce(f32[256]{0:T(256)S(1)} %get-tuple-element.20, f32[256]{0:T(256)S(1)} %get-tuple-element.14, f32[256]{0:T(256)S(1)} %get-tuple-element.18), channel_id=1, replica_groups=mesh['tok'=8,'wid'=64] {'tok'}, use_global_device_ids=true, to_apply=%region_5.7 | all-reduce | flops 768 | bytes 6144 | tf_op jit(solution)/shard_map/psum | solution.py:62
  295.9 14.7 %all-reduce = (f32[256]{0:T(256)S(1)}, f32[256]{0:T(256)S(1)}, f32[256]{0:T(256)S(1)}) all-reduce(f32[256]{0:T(256)S(1)} %get-tuple-element.28, f32[256]{0:T(256)S(1)} %get-tuple-element.29, f32[256]{0:T(256)S(1)} %multiply_reduce_fusion.2), channel_id=1, replica_groups=mesh['tok'=8,'wid'=64] {'tok'}, use_global_device_ids=true, to_apply=%region_11.13 | all-reduce | flops 768 | bytes 6144 | tf_op jit(solution)/shard_map/psum | solution.py:66
  310.7 11.2 %all-gather.17.cloned.1.call-done = bf16[256,4096]{0,1:T(8,128)(2,1)} async-done(((bf16[256,512]{0,1:T(8,128)(2,1)}), bf16[256,4096]{0,1:T(8,128)(2,1)}) %all-gather.17.cloned.1.call-update) | async-done | bytes 2097168 | tf_op jit(solution)/shard_map/all_gather | solution.py:86
  321.9 4.3 fusion.2
  326.2 150.6 %reduce-scatter.2.cloned.1.call-done = f32[192,64]{0,1:T(8,128)} async-done(((f32[192,4096]{0,1:T(8,128)}), f32[192,64]{0,1:T(8,128)}) %reduce-scatter.2.cloned.1.call-update) | async-done | bytes 49168 | tf_op jit(solution)/shard_map/reduce_scatter | solution.py:89
  476.8 1.5 convert_element_type.27
  (33 shorter events, 2.7 us)
Async XLA Ops:
  6.5 32.5 %copy-start.1 = (bf16[256,512]{1,0:T(8,128)(2,1)S(1)}, bf16[256,512]{1,0:T(8,128)(2,1)}, u32[]{:S(2)}) copy-start(bf16[256,512]{1,0:T(8,128)(2,1)} %param.16) | copy-start | bytes 786436
  6.5 50.9 %copy-start.3 = (s32[128]{0:T(128)S(1)}, s32[128]{0:T(128)}, u32[]{:S(2)}) copy-start(s32[128]{0:T(128)} %param.17) | copy-start | bytes 1540
  6.5 120.6 %all-gather.7.cloned.1.call-start = ((), (), s32[]{:S(2)}) async-start(), calls=%async_computation.7 | async-start | bytes 2129920 | tf_op jit(solution)/shard_map/all_gather | solution.py:31
  7.3 136.1 %all-gather.9.cloned.1.call-start = ((), (), s32[]{:S(2)}) async-start(), calls=%async_computation.8 | async-start | bytes 2359296 | tf_op jit(solution)/shard_map/all_gather | solution.py:51
  8.0 180.2 %all-gather.13.cloned.1.call-start = ((), (), s32[]{:S(2)}) async-start(), calls=%async_computation.10 | async-start | bytes 2359296 | tf_op jit(solution)/shard_map/all_gather | solution.py:52
  10.5 22.2 %all-to-all-start = ((bf16[256,64,8]{0,2,1:T(8,128)(2,1)}), bf16[256,64,8]{0,2,1:T(8,128)(2,1)S(1)}, u32[]{:S(2)}, u32[]{:S(2)}) async-start(bf16[256,64,8]{0,2,1:T(8,128)(2,1)} %bitcast), calls=%async_computation | async-start | bytes 524288 | tf_op jit(solution)/shard_map/all_to_all | solution.py:34
  32.7 18.0 %all-to-all-start.2 = ((bf16[256,64,8]{0,2,1:T(8,128)(2,1)}), bf16[256,64,8]{0,2,1:T(8,128)(2,1)S(1)}, u32[]{:S(2)}, u32[]{:S(2)}) async-start(bf16[256,64,8]{0,2,1:T(8,128)(2,1)} %bitcast.7), calls=%async_computation.2 | async-start | bytes 524288 | tf_op jit(solution)/shard_map/all_to_all | solution.py:35
  50.7 18.4 %all-to-all-start.4 = ((bf16[256,64,8]{0,2,1:T(8,128)(2,1)}), bf16[256,64,8]{0,2,1:T(8,128)(2,1)S(1)}, u32[]{:S(2)}, u32[]{:S(2)}) async-start(bf16[256,64,8]{0,2,1:T(8,128)(2,1)} %bitcast.14), calls=%async_computation.4 | async-start | bytes 524288 | tf_op jit(solution)/shard_map/all_to_all | solution.py:36
  57.4 175.5 %all-gather.11.cloned.1.call-start = ((), (), s32[]{:S(2)}) async-start(), calls=%async_computation.9 | async-start | bytes 2359296 | tf_op jit(solution)/shard_map/all_gather | solution.py:53
  69.8 44.8 %copy-start.2 = (bf16[256,512]{1,0:T(8,128)(2,1)S(1)}, bf16[256,512]{1,0:T(8,128)(2,1)}, u32[]{:S(2)}) copy-start(bf16[256,512]{1,0:T(8,128)(2,1)} %param.15) | copy-start | bytes 786436
  89.8 187.7 %all-gather.15.cloned.1.call-start = ((), (), s32[]{:S(2)}) async-start(), calls=%async_computation.11 | async-start | bytes 2359296 | tf_op jit(solution)/shard_map/all_gather | solution.py:54
  108.2 18.0 %all-to-all-start.5 = ((bf16[64,256,8]{1,2,0:T(8,128)(2,1)}), bf16[64,256,8]{1,2,0:T(8,128)(2,1)S(1)}, u32[]{:S(2)}, u32[]{:S(2)}) async-start(bf16[64,256,8]{1,2,0:T(8,128)(2,1)} %bitcast.17), calls=%async_computation.5 | async-start | bytes 524288 | tf_op jit(solution)/shard_map/all_to_all | solution.py:45
  114.6 207.3 %all-gather.17.cloned.1.call-start = ((), (), s32[]{:S(2)}) async-start(), calls=%async_computation.12 | async-start | bytes 2359296 | tf_op jit(solution)/shard_map/all_gather | solution.py:86
  127.1 349.7 %reduce-scatter.2.cloned.1.call-start = ((), (), s32[]{:S(2)}) async-start(), calls=%async_computation.13 | async-start | bytes 4259840 | tf_op jit(solution)/shard_map/reduce_scatter | solution.py:89
  127.2 61.0 %copy-start = (bf16[192,4096]{0,1:T(8,128)(2,1)S(1)}, bf16[192,4096]{0,1:T(8,128)(2,1)}, u32[]{:S(2)}) copy-start(bf16[192,4096]{0,1:T(8,128)(2,1)} %all-gather.7.cloned.1.call-done) | copy-start | bytes 4718596
Sparse Core Ops, SparseCore 0:
  10.7 88.4 all-gather.6
  101.3 41.9 all-gather.8
  145.4 42.7 all-gather.12
  190.2 42.7 all-gather.10
  234.8 42.7 all-gather.14
  279.5 42.3 all-gather.16
  326.6 150.1 reduce-scatter.1
where the time goes:
time: 486 us; the launch traced here: 485 us
  waiting for transfers between devices  349 us (72%)
  blocking collectives  67.8 us (14%)
  starting transfers between devices  30 us (6%)
  matrix products  14.7 us (3%)
  between operations  13.6 us (3%)
  local copies, waits for them, and re-layouts  6.63 us (1%)
    reduce_scatter x1, waiting for transfers between devices, local(): lax.psum_scatter(partial_out, 'wid', scatter_dimension=1, tiled=True)  151 us
    all_gather x1, waiting for transfers between devices, local(): lax.all_gather(gate_src, 'tok', axis=1, tiled=True)  42.3 us
    all_gather x1, waiting for transfers between devices, local(): lax.all_gather(up_src, 'tok', axis=1, tiled=True)  42.2 us
    all_gather x1, waiting for transfers between devices, local(): lax.all_gather(up_a, 'tok', axis=1, tiled=True)  41.8 us
    all_to_all x1, blocking collectives, local(): lax.all_to_all(reorder_blocks(shipped[0], block_perm), 'wid', split_axis=...  19.1 us
    all_to_all x1, blocking collectives, local(): lax.all_to_all(reorder_blocks(shipped[1], block_perm), 'wid', split_axis=...  18.3 us
    all_gather x1, waiting for transfers between devices, local(): lax.all_gather(gate_a, 'tok', axis=1, tiled=True)  16.2 us
    psum x1, blocking collectives, local(): lax.psum((jnp.sum(hid_a, axis=0), jnp.sum(hid_b, axis=0), jnp.sum(hid_m,...  15.7 us
  transfers between devices with their start and end apart: 11, of which 10 were waited for; matrix products, arithmetic and copies ran while one was open for 4% of the time, Pallas kernels for 0%

commit v1 on v0

--- a/solution.py
+++ b/solution.py
@@ -31,7 +31,10 @@
     gathered = lax.all_gather(tokens, "wid", axis=1, tiled=True)
     row_count = gathered.shape[0]
     shipped = (
-        lax.all_to_all(gate_b, "wid", split_axis=1, concat_axis=0, tiled=True),
+        jnp.concatenate(
+            lax.all_to_all(jnp.stack(jnp.split(gate_b, lax.axis_size("wid"), axis=1)), "wid", 0, 0),
+            axis=0,
+        ),
         lax.all_to_all(up_b, "wid", split_axis=1, concat_axis=0, tiled=True),
         lax.all_to_all(down_b, "wid", split_axis=1, concat_axis=0, tiled=True),
     )

time: 486 us -> 487 us (level)
  local copies, waits for them, and re-layouts: 6.63 us -> 62.2 us
  waiting for transfers between devices: 349 us -> 294 us
    unnamed x12 -> x142, local copies, waits for them, and re-layouts: 4.56 us -> 55.9 us
    all_gather x1, waiting for transfers between devices: 41.8 us -> 0.99 us  [local(): lax.all_gather(up_a, 'tok', axis=1, tiled=True)]
    all_gather x1, waiting for transfers between devices: 16.2 us -> 0.02 us  [local(): lax.all_gather(gate_a, 'tok', axis=1, tiled=True)]
  transfers between devices with their start and end apart: 11 -> 11, of which waited for: 10 -> 9; matrix products, arithmetic and copies ran while one was open for 4% -> 15% of each run, Pallas kernels for 0% -> 0%
where the time goes in v1:
time: 487 us; the launch traced here: 485 us
  waiting for transfers between devices  294 us (60%)
  blocking collectives  66.3 us (14%)
  local copies, waits for them, and re-layouts  62.2 us (13%)
  starting transfers between devices  30.4 us (6%)
  matrix products  14.9 us (3%)
  between operations  13.8 us (3%)
    reduce_scatter x1, waiting for transfers between devices, local(): lax.psum_scatter(partial_out, 'wid', scatter_dimension=1, tiled=True)  151 us
    unnamed x142, local copies, waits for them, and re-layouts  55.9 us
    all_gather x1, waiting for transfers between devices, local(): lax.all_gather(gate_src, 'tok', axis=1, tiled=True)  42.7 us
    all_gather x1, waiting for transfers between devices, local(): lax.all_gather(up_src, 'tok', axis=1, tiled=True)  42.2 us
    all_to_all x1, blocking collectives, local(): lax.all_to_all(reorder_blocks(shipped[1], block_perm), 'wid', split_axis=...  17.9 us
    all_to_all x1, blocking collectives, local(): lax.all_to_all(reorder_blocks(shipped[0], block_perm), 'wid', split_axis=...  17.9 us
    psum x1, blocking collectives, local(): lax.psum((jnp.sum(hid_a, axis=0), jnp.sum(hid_b, axis=0), jnp.sum(hid_m,...  15.7 us
    psum x1, blocking collectives, local(): lax.psum((jnp.sum((hid_a - centers[0]) ** 2, axis=0), jnp.sum((hid_b - ce...  14.7 us
  transfers between devices with their start and end apart: 11, of which 9 were waited for; matrix products, arithmetic and copies ran while one was open for 15% of the time, Pallas kernels for 0%

profile of v1, /device:TPU:16, one launch (start us, length us, event | category | flops | bytes accessed | tf_op | source)
XLA Modules:
  0.0 485.2 jit_solution(18330942170350124329)
XLA Ops:
  8.7 1.6 fusion.13
  10.3 1.3 fusion.12
  13.6 0.9 copy.92
  14.5 0.9 copy.93
  16.3 0.9 copy.95
  20.9 0.9 copy.100
  22.7 0.9 copy.102
  25.4 1.0 copy.105
  67.1 10.5 %all-to-all-start = ((bf16[64,256,8]{1,2,0:T(8,128)(2,1)}), bf16[64,256,8]{1,2,0:T(8,128)(2,1)S(1)}, u32[]{:S(2)}, u32[]{:S(2)}) async-start(bf16[64,256,8]{1,2,0:T(8,128)(2,1)} %constant_dynamic-update-slice_fusion), calls=%async_computation | async-start | bytes 524288 | tf_op jit(solution)/shard_map/all_to_all | solution.py:35
  78.5 11.8 %all-to-all-done = bf16[64,256,8]{1,2,0:T(8,128)(2,1)S(1)} async-done(((bf16[64,256,8]{1,2,0:T(8,128)(2,1)}), bf16[64,256,8]{1,2,0:T(8,128)(2,1)S(1)}, u32[]{:S(2)}, u32[]{:S(2)}) %all-to-all-start) | async-done | bytes 262176 | tf_op jit(solution)/shard_map/all_to_all | solution.py:35
  90.2 6.9 %all-to-all-start.2 = ((bf16[256,64,8]{0,2,1:T(8,128)(2,1)}), bf16[256,64,8]{0,2,1:T(8,128)(2,1)S(1)}, u32[]{:S(2)}, u32[]{:S(2)}) async-start(bf16[256,64,8]{0,2,1:T(8,128)(2,1)} %bitcast.69), calls=%async_computation.2 | async-start | bytes 524288 | tf_op jit(solution)/shard_map/all_to_all | solution.py:38
  98.0 10.9 %all-to-all-done.2 = bf16[256,64,8]{0,2,1:T(8,128)(2,1)S(1)} async-done(((bf16[256,64,8]{0,2,1:T(8,128)(2,1)}), bf16[256,64,8]{0,2,1:T(8,128)(2,1)S(1)}, u32[]{:S(2)}, u32[]{:S(2)}) %all-to-all-start.2) | async-done | bytes 262176 | tf_op jit(solution)/shard_map/all_to_all | solution.py:38
  108.8 6.3 %all-to-all-start.4 = ((bf16[256,64,8]{0,2,1:T(8,128)(2,1)}), bf16[256,64,8]{0,2,1:T(8,128)(2,1)S(1)}, u32[]{:S(2)}, u32[]{:S(2)}) async-start(bf16[256,64,8]{0,2,1:T(8,128)(2,1)} %bitcast.76), calls=%async_computation.4 | async-start | bytes 524288 | tf_op jit(solution)/shard_map/all_to_all | solution.py:39
  116.6 10.2 %all-to-all-done.4 = bf16[256,64,8]{0,2,1:T(8,128)(2,1)S(1)} async-done(((bf16[256,64,8]{0,2,1:T(8,128)(2,1)}), bf16[256,64,8]{0,2,1:T(8,128)(2,1)S(1)}, u32[]{:S(2)}, u32[]{:S(2)}) %all-to-all-start.4) | async-done | bytes 262176 | tf_op jit(solution)/shard_map/all_to_all | solution.py:39
  127.6 0.9 broadcast_select_fusion.2
  128.5 17.9 %all_to_all.88 = bf16[64,256,8]{1,2,0:T(8,128)(2,1)} all-to-all(bf16[64,256,8]{1,2,0:T(8,128)(2,1)S(1)} %bitcast.173), channel_id=1, replica_groups=mesh['tok'=8,'wid'=64] {'wid'}, dimensions={0} | all-to-all | bytes 524288 | tf_op jit(solution)/shard_map/all_to_all | solution.py:42
  146.5 17.9 %all_to_all.89 = bf16[64,256,8]{1,2,0:T(8,128)(2,1)} all-to-all(bf16[64,256,8]{1,2,0:T(8,128)(2,1)S(1)} %bitcast.172), channel_id=1, replica_groups=mesh['tok'=8,'wid'=64] {'wid'}, dimensions={0} | all-to-all | bytes 524288 | tf_op jit(solution)/shard_map/all_to_all | solution.py:45
  164.5 6.3 %all-to-all-start.5 = ((bf16[64,256,8]{1,2,0:T(8,128)(2,1)}), bf16[64,256,8]{1,2,0:T(8,128)(2,1)S(1)}, u32[]{:S(2)}, u32[]{:S(2)}) async-start(bf16[64,256,8]{1,2,0:T(8,128)(2,1)} %bitcast.79), calls=%async_computation.5 | async-start | bytes 524288 | tf_op jit(solution)/shard_map/all_to_all | solution.py:48
  171.0 11.5 %all-to-all-done.5 = bf16[64,256,8]{1,2,0:T(8,128)(2,1)S(1)} async-done(((bf16[64,256,8]{1,2,0:T(8,128)(2,1)}), bf16[64,256,8]{1,2,0:T(8,128)(2,1)S(1)}, u32[]{:S(2)}, u32[]{:S(2)}) %all-to-all-start.5) | async-done | bytes 262176 | tf_op jit(solution)/shard_map/all_to_all | solution.py:48
  183.6 3.2 fusion.14
  186.9 1.0 all-gather.13.cloned.1.call-done
  187.9 2.4 fusion.15
  190.3 42.7 %all-gather.11.cloned.1.call-done = bf16[256,4096]{0,1:T(8,128)(2,1)} async-done(((bf16[256,512]{0,1:T(8,128)(2,1)}), bf16[256,4096]{0,1:T(8,128)(2,1)}) %all-gather.11.cloned.1.call-update) | async-done | bytes 2097168 | tf_op jit(solution)/shard_map/all_gather | solution.py:56
  233.0 2.4 convolution_bitcast_fusion.1
  235.5 42.2 %all-gather.15.cloned.1.call-done = bf16[256,4096]{0,1:T(8,128)(2,1)} async-done(((bf16[256,512]{0,1:T(8,128)(2,1)}), bf16[256,4096]{0,1:T(8,128)(2,1)}) %all-gather.15.cloned.1.call-update) | async-done | bytes 2097168 | tf_op jit(solution)/shard_map/all_gather | solution.py:57
  277.7 2.5 fusion.8
  280.3 15.7 %all-reduce.1 = (f32[256]{0:T(256)S(1)}, f32[256]{0:T(256)S(1)}, f32[256]{0:T(256)S(1)}) all-reduce(f32[256]{0:T(256)S(1)} %get-tuple-element.20, f32[256]{0:T(256)S(1)} %get-tuple-element.14, f32[256]{0:T(256)S(1)} %get-tuple-element.18), channel_id=1, replica_groups=mesh['tok'=8,'wid'=64] {'tok'}, use_global_device_ids=true, to_apply=%region_5.7 | all-reduce | flops 768 | bytes 6144 | tf_op jit(solution)/shard_map/psum | solution.py:65
  296.1 14.7 %all-reduce = (f32[256]{0:T(256)S(1)}, f32[256]{0:T(256)S(1)}, f32[256]{0:T(256)S(1)}) all-reduce(f32[256]{0:T(256)S(1)} %get-tuple-element.92, f32[256]{0:T(256)S(1)} %get-tuple-element.93, f32[256]{0:T(256)S(1)} %multiply_reduce_fusion.2), channel_id=1, replica_groups=mesh['tok'=8,'wid'=64] {'tok'}, use_global_device_ids=true, to_apply=%region_11.13 | all-reduce | flops 768 | bytes 6144 | tf_op jit(solution)/shard_map/psum | solution.py:69
  310.8 11.2 %all-gather.17.cloned.1.call-done = bf16[256,4096]{0,1:T(8,128)(2,1)} async-done(((bf16[256,512]{0,1:T(8,128)(2,1)}), bf16[256,4096]{0,1:T(8,128)(2,1)}) %all-gather.17.cloned.1.call-update) | async-done | bytes 2097168 | tf_op jit(solution)/shard_map/all_gather | solution.py:89
  322.0 4.3 fusion.2
  326.3 150.6 %reduce-scatter.2.cloned.1.call-done = f32[192,64]{0,1:T(8,128)} async-done(((f32[192,4096]{0,1:T(8,128)}), f32[192,64]{0,1:T(8,128)}) %reduce-scatter.2.cloned.1.call-update) | async-done | bytes 49168 | tf_op jit(solution)/shard_map/reduce_scatter | solution.py:92
  476.9 1.5 convert_element_type.27
  (168 shorter events, 57.4 us)
Async XLA Ops:
  6.5 3.8 copy-start
  6.5 177.0 %all-gather.7.cloned.1.call-start = ((), (), s32[]{:S(2)}) async-start(), calls=%async_computation.7 | async-start | bytes 2129920 | tf_op jit(solution)/shard_map/all_gather | solution.py:31
  7.3 176.4 %all-gather.9.cloned.1.call-start = ((), (), s32[]{:S(2)}) async-start(), calls=%async_computation.8 | async-start | bytes 2359296 | tf_op jit(solution)/shard_map/all_gather | solution.py:54
  8.0 179.8 %all-gather.13.cloned.1.call-start = ((), (), s32[]{:S(2)}) async-start(), calls=%async_computation.10 | async-start | bytes 2359296 | tf_op jit(solution)/shard_map/all_gather | solution.py:55
  25.4 52.2 %copy-start.2 = (bf16[256,512]{1,0:T(8,128)(2,1)S(1)}, bf16[256,512]{1,0:T(8,128)(2,1)}, u32[]{:S(2)}) copy-start(bf16[256,512]{1,0:T(8,128)(2,1)} %param.14) | copy-start | bytes 786436
  27.5 69.6 %copy-start.3 = (bf16[256,512]{1,0:T(8,128)(2,1)S(1)}, bf16[256,512]{1,0:T(8,128)(2,1)}, u32[]{:S(2)}) copy-start(bf16[256,512]{1,0:T(8,128)(2,1)} %param.16) | copy-start | bytes 786436
  28.7 86.5 %copy-start.5 = (s32[128]{0:T(128)S(1)}, s32[128]{0:T(128)}, u32[]{:S(2)}) copy-start(s32[128]{0:T(128)} %param.17) | copy-start | bytes 1540
  67.1 23.1 %all-to-all-start = ((bf16[64,256,8]{1,2,0:T(8,128)(2,1)}), bf16[64,256,8]{1,2,0:T(8,128)(2,1)S(1)}, u32[]{:S(2)}, u32[]{:S(2)}) async-start(bf16[64,256,8]{1,2,0:T(8,128)(2,1)} %constant_dynamic-update-slice_fusion), calls=%async_computation | async-start | bytes 524288 | tf_op jit(solution)/shard_map/all_to_all | solution.py:35
  90.2 18.6 %all-to-all-start.2 = ((bf16[256,64,8]{0,2,1:T(8,128)(2,1)}), bf16[256,64,8]{0,2,1:T(8,128)(2,1)S(1)}, u32[]{:S(2)}, u32[]{:S(2)}) async-start(bf16[256,64,8]{0,2,1:T(8,128)(2,1)} %bitcast.69), calls=%async_computation.2 | async-start | bytes 524288 | tf_op jit(solution)/shard_map/all_to_all | solution.py:38
  108.8 18.0 %all-to-all-start.4 = ((bf16[256,64,8]{0,2,1:T(8,128)(2,1)}), bf16[256,64,8]{0,2,1:T(8,128)(2,1)S(1)}, u32[]{:S(2)}, u32[]{:S(2)}) async-start(bf16[256,64,8]{0,2,1:T(8,128)(2,1)} %bitcast.76), calls=%async_computation.4 | async-start | bytes 524288 | tf_op jit(solution)/shard_map/all_to_all | solution.py:39
  115.2 117.9 %all-gather.11.cloned.1.call-start = ((), (), s32[]{:S(2)}) async-start(), calls=%async_computation.9 | async-start | bytes 2359296 | tf_op jit(solution)/shard_map/all_gather | solution.py:56
  127.6 43.3 %copy-start.4 = (bf16[256,512]{1,0:T(8,128)(2,1)S(1)}, bf16[256,512]{1,0:T(8,128)(2,1)}, u32[]{:S(2)}) copy-start(bf16[256,512]{1,0:T(8,128)(2,1)} %param.15) | copy-start | bytes 786436
  146.4 131.3 %all-gather.15.cloned.1.call-start = ((), (), s32[]{:S(2)}) async-start(), calls=%async_computation.11 | async-start | bytes 2359296 | tf_op jit(solution)/shard_map/all_gather | solution.py:57
  164.5 18.0 %all-to-all-start.5 = ((bf16[64,256,8]{1,2,0:T(8,128)(2,1)}), bf16[64,256,8]{1,2,0:T(8,128)(2,1)S(1)}, u32[]{:S(2)}, u32[]{:S(2)}) async-start(bf16[64,256,8]{1,2,0:T(8,128)(2,1)} %bitcast.79), calls=%async_computation.5 | async-start | bytes 524288 | tf_op jit(solution)/shard_map/all_to_all | solution.py:48
  170.8 151.2 %all-gather.17.cloned.1.call-start = ((), (), s32[]{:S(2)}) async-start(), calls=%async_computation.12 | async-start | bytes 2359296 | tf_op jit(solution)/shard_map/all_gather | solution.py:89
  183.3 293.6 %reduce-scatter.2.cloned.1.call-start = ((), (), s32[]{:S(2)}) async-start(), calls=%async_computation.13 | async-start | bytes 4259840 | tf_op jit(solution)/shard_map/reduce_scatter | solution.py:92
  183.6 4.3 copy-start.1
Sparse Core Ops, SparseCore 0:
  10.7 87.8 all-gather.6
  100.7 42.7 all-gather.8
  145.6 42.2 all-gather.12
  189.8 43.2 all-gather.10
  235.0 42.7 all-gather.14
  279.7 42.3 all-gather.16
  326.7 150.1 reduce-scatter.1
